TPU v7x, 1024 devices: a whole 8x8x8 slice. The times are simulated.
1024 devices in a mesh: replica: 8 (over y_hi, core), shard: 128 (over z, x, y_lo).
Axes of the slice: x: 8, y: 8 (y_hi: 4, y_lo: 2; y = y_hi * 2 + y_lo), z: 8, core: 2. Of those that a mesh axis runs over, the one named last changes fastest.
Arguments:
- tokens_in: bfloat16 [131072, 8192], P(('replica', 'shard')), may hold values from -24 to 24
- cotangent: bfloat16 [131072, 128], P(('replica', 'shard')), may hold values from -0.03125 to 0.03125
- next_tokens: bfloat16 [65536, 8192], P(('replica', 'shard')), may hold values from -24 to 24
- master: float32 [8192, 128], P(('replica', 'shard')), may hold values from -0.0625 to 0.0625
- first_moment: float32 [8192, 128], P(('replica', 'shard')), may hold values from -6 to 6
- second_moment: float32 [8192, 128], P(('replica', 'shard')), may hold values from 0.25 to 4
Outputs:
- new_master: float32 [8192, 128], P(('replica', 'shard'))
- new_first: float32 [8192, 128], P(('replica', 'shard'))
- new_second: float32 [8192, 128], P(('replica', 'shard'))
- next_out: bfloat16 [65536, 128], P(('replica', 'shard'))
All inputs are finite; a program needn't handle non-finite values.
Results may differ from a plain program's by a relative error of at most 0.005.
Values may be sent and summed in bfloat16 or wider, within the bound.
No kernel may reach another device: no remote copies, remote signals or barrier semaphores. Data moves between devices by JAX's collectives and lax.ppermute only.
A program may use at most 32 MiB of HBM per device.

v0:
```python
import jax
import jax.numpy as jnp
from jax import lax
from jax.sharding import PartitionSpec as P

beta_one = 0.9
beta_two = 0.95
learn_rate = 0.003
decay_rate = 0.1
epsilon = 1e-08
steps_done = 10


def on_device(tokens_in, cotangent, next_tokens, master, first_moment, second_moment):
    n_rep = lax.axis_size("replica")
    n_shard = lax.axis_size("shard")
    model_width = tokens_in.shape[1]
    own_rows = model_width // (n_rep * n_shard)

    def permute(matrix):
        row_count = matrix.shape[0]
        arranged = matrix.reshape(row_count, n_rep, n_shard, own_rows).transpose(0, 2, 1, 3)
        return arranged.reshape(row_count, model_width)

    piece = permute(tokens_in)
    grouped = lax.psum_scatter(
        lax.dot_general(
            piece, cotangent, (((0,), (0,)), ((), ())), preferred_element_type=jnp.float32
        ),
        "shard",
        scatter_dimension=0,
        tiled=True,
    )
    gradient = lax.psum_scatter(grouped, "replica", scatter_dimension=0, tiled=True)
    new_first = beta_one * first_moment + (1.0 - beta_one) * gradient
    new_second = beta_two * second_moment + (1.0 - beta_two) * gradient * gradient
    first_hat = new_first / (1.0 - beta_one**steps_done)
    second_hat = new_second / (1.0 - beta_two**steps_done)
    new_master = master - learn_rate * (
        first_hat / (jnp.sqrt(second_hat) + epsilon) + decay_rate * master
    )
    low_weight = new_master.astype(jnp.bfloat16)
    group_rows = lax.all_gather(low_weight, "replica", axis=0, tiled=True)
    columns = permute(next_tokens)
    summed = jnp.dot(
        columns,
        lax.all_gather(group_rows, "shard", axis=0, tiled=True),
        preferred_element_type=jnp.float32,
    )
    next_out = summed.astype(jnp.bfloat16)
    return (new_master, new_first, new_second, next_out)


def solution(mesh):
    in_specs = (
        P(("replica", "shard"), None),
        P(("replica", "shard"), None),
        P(("replica", "shard"), None),
        P(("replica", "shard"), None),
        P(("replica", "shard"), None),
        P(("replica", "shard"), None),
    )
    out_specs = (
        P(("replica", "shard"), None),
        P(("replica", "shard"), None),
        P(("replica", "shard"), None),
        P(("replica", "shard"), None),
    )
    return jax.shard_map(
        on_device, mesh=mesh, in_specs=in_specs, out_specs=out_specs, check_vma=False
    )
```

profile of v0, /device:TPU:32, one launch (start us, length us, event | category | flops | bytes accessed | tf_op | source)
XLA Modules:
  0.0 1303.2 jit_solution(9247026997918998554)
XLA Ops:
  7.2 0.0 copy-start
  7.2 0.0 reduce-scatter.2.cloned.1.call-start
  7.2 3.2 copy.14
  10.5 0.6 copy.15
  11.1 0.0 copy-done
  11.1 2.6 fusion.4
  13.7 0.0 copy-start.2
  13.7 0.0 copy-start.3
  13.7 0.0 copy-start.4
  13.7 0.0 copy-start.1
  13.7 0.0 reduce-scatter.2.cloned.1.call-update
  13.7 0.0 all-gather.2.cloned.1.call-start
  13.8 1.4 dynamic-slice
  15.8 648.4 %reduce-scatter.2.cloned.1.call-done = f32[64,128]{1,0:T(8,128)} async-done(((f32[8192,128]{1,0:T(8,128)}), f32[64,128]{1,0:T(8,128)}) %reduce-scatter.2.cloned.1.call-update) | async-done | bytes 32784 | tf_op jit(solution)/shard_map/reduce_scatter | solution.py:26
  664.2 24.6 %all-reduce = f32[64,128]{1,0:T(8,128)S(1)} all-reduce(f32[64,128]{1,0:T(8,128)} %reduce-scatter.2.cloned.1.call-done), channel_id=3, replica_groups=mesh['replica'=8,'shard'=128] {'replica'}, use_global_device_ids=true, to_apply=%region_1.0.clone | all-reduce | flops 8192 | bytes 65536
  688.8 0.0 copy-done.2
  688.8 0.0 copy-done.3
  688.9 0.0 copy-done.4
  688.9 0.6 fusion.2
  689.5 15.8 %all_gather.6 = bf16[64,128]{1,0:T(8,128)(2,1)} all-gather(bf16[8,128]{1,0:T(8,128)(2,1)S(1)} %get-tuple-element.4), channel_id=1, replica_groups=mesh['replica'=8,'shard'=128] {'replica'}, dimensions={0}, use_global_device_ids=true | all-gather | bytes 18432 | tf_op jit(solution)/shard_map/all_gather | solution.py:43
  705.3 0.0 all-gather.2.cloned.1.call-update
  705.4 0.0 copy-done.1
  705.4 1.8 copy.16
  707.2 2.2 copy.17
  709.3 584.0 %all-gather.2.cloned.1.call-done = bf16[8192,128]{1,0:T(8,128)(2,1)} async-done(((bf16[64,128]{1,0:T(8,128)(2,1)}), bf16[8192,128]{1,0:T(8,128)(2,1)}) %all-gather.2.cloned.1.call-update) | async-done | bytes 2097168 | tf_op jit(solution)/shard_map/all_gather | solution.py:47
  1293.3 3.1 fusion
Async XLA Ops:
  7.2 3.9 copy-start
  7.2 657.0 %reduce-scatter.2.cloned.1.call-start = ((), (), s32[]{:S(2)}) async-start(), calls=%async_computation.1 | async-start | bytes 4227072 | tf_op jit(solution)/shard_map/reduce_scatter | solution.py:26
  13.7 675.1 %copy-start.2 = (f32[8,128]{1,0:T(8,128)S(1)}, f32[8,128]{1,0:T(8,128)}, u32[]{:S(2)}) copy-start(f32[8,128]{1,0:T(8,128)} %param.9) | copy-start | bytes 12292
  13.7 675.1 %copy-start.3 = (f32[8,128]{1,0:T(8,128)S(1)}, f32[8,128]{1,0:T(8,128)}, u32[]{:S(2)}) copy-start(f32[8,128]{1,0:T(8,128)} %param.10) | copy-start | bytes 12292
  13.7 675.2 %copy-start.4 = (f32[8,128]{1,0:T(8,128)S(1)}, f32[8,128]{1,0:T(8,128)}, u32[]{:S(2)}) copy-start(f32[8,128]{1,0:T(8,128)} %param.11) | copy-start | bytes 12292
  13.7 691.7 %copy-start.1 = (bf16[64,8192]{1,0:T(8,128)(2,1)S(1)}, bf16[64,8192]{1,0:T(8,128)(2,1)}, u32[]{:S(2)}) copy-start(bf16[64,8192]{1,0:T(8,128)(2,1)} %param.8) | copy-start | bytes 3145732
  13.7 1279.6 %all-gather.2.cloned.1.call-start = ((), (), s32[]{:S(2)}) async-start(), calls=%async_computation.2 | async-start | bytes 2113536 | tf_op jit(solution)/shard_map/all_gather | solution.py:47
Sparse Core Ops, SparseCore 0:
  13.9 650.3 reduce-scatter.1
  705.5 587.8 all-gather.1
where the time goes:
time: 1300 us
  waiting for transfers between devices  1230 us (95%)
  blocking collectives  40.5 us (3%)
  between operations  14.8 us (1%)
    reduce_scatter x1, waiting for transfers between devices, on_device(): lax.psum_scatter(lax.dot_general(piece, cotangent, (((0,), (0,)), ((), ()...  648 us
    all_gather x1, waiting for transfers between devices, on_device(): lax.all_gather(group_rows, 'shard', axis=0, tiled=True)  584 us
  transfers between devices with their start and end apart: 2, of which 2 were waited for; matrix products, arithmetic and copies ran while one was open for 0% of the time, Pallas kernels for 0%

commit v1 on v0

v1 whole, which is shorter than its diff:
```python
import jax
import jax.numpy as jnp
from jax import lax
from jax.sharding import Mesh, PartitionSpec as P

beta_one = 0.9
beta_two = 0.95
learn_rate = 0.003
decay_rate = 0.1
epsilon = 1e-08
steps_done = 10

AXES = ("yh", "c", "zh", "zl", "xh", "xl", "yl")
NEAR = ("zl", "xl", "yl")
FAR = ("yh", "zh", "xh")


def on_device(tokens_in, cotangent, next_tokens, master, first_moment, second_moment):
    sizes = [lax.axis_size(a) for a in AXES]
    n_near = lax.axis_size(NEAR)
    n_far = lax.axis_size(FAR)
    model_width = tokens_in.shape[1]
    cols = cotangent.shape[1]
    own_rows = model_width // lax.axis_size(AXES)
    core = lax.axis_index("c")
    swap = [(0, 1), (1, 0)]

    gradient = lax.dot_general(
        tokens_in, cotangent, (((0,), (0,)), ((), ())), preferred_element_type=jnp.float32
    )
    split = gradient.reshape(*sizes, own_rows, cols).transpose(1, 3, 5, 6, 0, 2, 4, 7, 8)
    split = split.reshape(2, n_near, n_far * own_rows, cols)
    keep = lax.dynamic_index_in_dim(split, core, 0, keepdims=False)
    give = lax.dynamic_index_in_dim(split, 1 - core, 0, keepdims=False)
    got = lax.ppermute(give.astype(jnp.bfloat16), "c", swap)
    pair = (keep + got.astype(jnp.float32)).astype(jnp.bfloat16)
    near = lax.all_to_all(pair, NEAR, 0, 0, tiled=True)
    near = jnp.sum(near.astype(jnp.float32), axis=0).astype(jnp.bfloat16)
    far = lax.all_to_all(near.reshape(n_far, own_rows, cols), FAR, 0, 0, tiled=True)
    gradient = jnp.sum(far.astype(jnp.float32), axis=0)

    new_first = beta_one * first_moment + (1.0 - beta_one) * gradient
    new_second = beta_two * second_moment + (1.0 - beta_two) * gradient * gradient
    first_hat = new_first / (1.0 - beta_one**steps_done)
    second_hat = new_second / (1.0 - beta_two**steps_done)
    new_master = master - learn_rate * (
        first_hat / (jnp.sqrt(second_hat) + epsilon) + decay_rate * master
    )
    low_weight = new_master.astype(jnp.bfloat16)

    far = jnp.broadcast_to(low_weight, (n_far, own_rows, cols))
    far = lax.all_to_all(far, FAR, 0, 0, tiled=True).reshape(n_far * own_rows, cols)
    near = jnp.broadcast_to(far, (n_near, n_far * own_rows, cols))
    near = lax.all_to_all(near, NEAR, 0, 0, tiled=True)
    other = lax.ppermute(near, "c", swap)

    by_owner = [sizes[3], sizes[5], sizes[6], sizes[0], sizes[2], sizes[4]]

    def natural(half):
        half = half.reshape(*by_owner, own_rows, cols)
        half = half.transpose(3, 4, 0, 5, 1, 2, 6, 7)
        return half.reshape(sizes[0], model_width // sizes[0] // 2, cols)

    tokens = next_tokens.reshape(-1, sizes[0], 2, model_width // sizes[0] // 2)
    own_tokens = lax.dynamic_index_in_dim(tokens, core, 2, keepdims=False)
    other_tokens = lax.dynamic_index_in_dim(tokens, 1 - core, 2, keepdims=False)
    contract = (((1, 2), (0, 1)), ((), ()))
    summed = lax.dot_general(
        own_tokens, natural(near), contract, preferred_element_type=jnp.float32
    ) + lax.dot_general(
        other_tokens, natural(other), contract, preferred_element_type=jnp.float32
    )
    next_out = summed.astype(jnp.bfloat16)
    return (new_master, new_first, new_second, next_out)


def solution(mesh):
    fine = Mesh(mesh.devices.reshape(4, 2, 4, 2, 4, 2, 2), AXES)
    spec = P(AXES, None)
    return jax.shard_map(
        on_device, mesh=fine, in_specs=(spec,) * 6, out_specs=(spec,) * 4, check_vma=False
    )
```

time: 1300 us -> 130 us (0.10)
  the two profiles are of different devices: /device:TPU:32 before, /device:TPU:1 now
where the time goes in v1:
time: 130 us
  blocking collectives  82.9 us (64%)
  starting transfers between devices  22.7 us (17%)
  local copies, waits for them, and re-layouts  14.6 us (11%)
  matrix products  3.55 us (3%)
  other arithmetic  2.64 us (2%)
  waiting for transfers between devices  2.48 us (2%)
    all_to_all x1, blocking collectives, on_device(): lax.all_to_all(near.reshape(n_far, own_rows, cols), FAR, 0, 0, tiled=True)  30.8 us
    all_to_all x1, blocking collectives, on_device(): lax.all_to_all(far, FAR, 0, 0, tiled=True).reshape(n_far * own_rows, cols)  19.5 us
    all_to_all x1, blocking collectives, on_device(): near = lax.all_to_all(pair, NEAR, 0, 0, tiled=True)  17.5 us
    ppermute x1, starting transfers between devices, on_device(): got = lax.ppermute(give.astype(jnp.bfloat16), 'c', swap)  16 us
    all_to_all x1, blocking collectives, on_device(): near = lax.all_to_all(near, NEAR, 0, 0, tiled=True)  15 us
    ppermute x1, starting transfers between devices, on_device(): other = lax.ppermute(near, 'c', swap)  6.67 us
    transpose x2, local copies, waits for them, and re-layouts, natural(): half = half.transpose(3, 4, 0, 5, 1, 2, 6, 7)  2.99 us
    dynamic_slice x1, local copies, waits for them, and re-layouts, on_device(): other_tokens = lax.dynamic_index_in_dim(tokens, 1 - core, 2, keepdims=False)  2.74 us
  transfers between devices with their start and end apart: 2, of which 1 were waited for; matrix products, arithmetic and copies ran while one was open for 5% of the time, Pallas kernels for 0%

profile of v1, /device:TPU:1, one launch (start us, length us, event | category | flops | bytes accessed | tf_op | source)
XLA Modules:
  0.0 129.6 jit_solution(1752108226673098624)
XLA Ops:
  0.6 0.0 copy-start
  0.6 1.6 %copy-done = bf16[128,8192]{1,0:T(8,128)(2,1)S(1)} copy-done((bf16[128,8192]{1,0:T(8,128)(2,1)S(1)}, bf16[128,8192]{1,0:T(8,128)(2,1)}, u32[]{:S(2)}) %copy-start) | copy-done | bytes 2097176
  2.2 1.5 %fusion.7 = f32[8192,128]{1,0:T(8,128)S(1)} fusion(bf16[128,8192]{1,0:T(8,128)(2,1)S(1)} %copy-done, bf16[128,128]{1,0:T(8,128)(2,1)} %param.7), kind=kOutput, calls=%fused_computation.18 | convolution fusion | flops 268435456 | bytes 6324224 | tf_op jit(solution)/shard_map/dot_general | solution.py:28
  3.7 2.5 %copy.17 = f32[4,2,4,2,4,2,2,8,128]{8,7,4,2,0,6,5,3,1:T(8,128)} copy(f32[4,2,4,2,4,2,2,8,128]{8,7,6,5,4,3,2,1,0:T(8,128)S(1)} %bitcast.38) | data formatting | bytes 8388608 | tf_op jit(solution)/shard_map/reshape | solution.py:31
  6.3 2.7 %fusion.3 = bf16[8,512,128]{2,1,0:T(8,128)(2,1)} fusion(f32[2,8,512,128]{3,2,1,0:T(8,128)} %bitcast.39, s32[]{:T(128)S(6)} %select_n.11), kind=kLoop, calls=%fused_computation.7 | loop fusion | bytes 2097156 | tf_op jit(solution)/shard_map/convert_element_type | solution.py:35
  9.0 16.0 %collective-permute-start = (bf16[8,512,128]{2,1,0:T(8,128)(2,1)}, bf16[8,512,128]{2,1,0:T(8,128)(2,1)S(1)}, u32[]{:S(2)}, u32[]{:S(2)}) collective-permute-start(bf16[8,512,128]{2,1,0:T(8,128)(2,1)} %fusion.3), channel_id=1, source_target_pairs={{0,128},{128,0},{1,129},{129,1},{2,130},{130,2},{3,131},{131,3},{4... | collective-permute-start | bytes 3145736 | tf_op jit(solution)/shard_map/ppermute | solution.py:35
  25.0 2.5 %collective-permute-done = bf16[8,512,128]{2,1,0:T(8,128)(2,1)S(1)} collective-permute-done((bf16[8,512,128]{2,1,0:T(8,128)(2,1)}, bf16[8,512,128]{2,1,0:T(8,128)(2,1)S(1)}, u32[]{:S(2)}, u32[]{:S(2)}) %collective-permute-start) | collective-permute-done | bytes 1048608 | tf_op jit(solution)/shard_map/ppermute | solution.py:35
  27.5 1.8 %fusion = bf16[8,512,128]{2,1,0:T(8,128)(2,1)S(1)} fusion(bf16[8,512,128]{2,1,0:T(8,128)(2,1)S(1)} %collective-permute-done, f32[2,8,512,128]{3,2,1,0:T(8,128)} %bitcast.40, s32[]{:T(128)S(6)} %select_n.10), kind=kLoop, calls=%fused_computation.1 | loop fusion | flops 1572864 | bytes 4194308 | tf_op jit(solution)/shard_map/convert_element_type | solution.py:36
  29.3 0.0 copy-start.1
  29.3 0.0 copy-start.2
  29.3 0.0 copy-start.3
  29.3 17.5 %all_to_all.20 = bf16[8,512,128]{2,1,0:T(8,128)(2,1)S(1)} all-to-all(bf16[8,512,128]{2,1,0:T(8,128)(2,1)S(1)} %fusion), channel_id=1, replica_groups=mesh['yh'=4,'c'=2,'zh'=4,'zl'=2,'xh'=4,'xl'=2,'yl'=2] {'zl','xl','yl'}, dimensions={0} | all-to-all | bytes 2097152 | tf_op jit(solution)/shard_map/all_to_all | solution.py:37
  46.9 0.1 reduce_sum.21
  47.0 30.8 %all_to_all.21 = bf16[64,8,128]{2,1,0:T(8,128)(2,1)S(1)} all-to-all(bf16[64,8,128]{2,1,0:T(8,128)(2,1)S(1)} %bitcast.43), channel_id=1, replica_groups=mesh['yh'=4,'c'=2,'zh'=4,'zl'=2,'xh'=4,'xl'=2,'yl'=2] {'yh','zh','xh'}, dimensions={0} | all-to-all | bytes 262144 | tf_op jit(solution)/shard_map/all_to_all | solution.py:39
  77.8 0.1 convert_reduce_fusion
  77.9 0.0 copy-done.1
  77.9 0.0 copy-done.2
  77.9 0.0 copy-done.3
  77.9 0.6 fusion.5
  78.5 19.5 %all_to_all.22 = bf16[64,8,128]{2,1,0:T(8,128)(2,1)S(1)} all-to-all(bf16[64,8,128]{2,1,0:T(8,128)(2,1)S(1)} %broadcast_in_dim.6), channel_id=1, replica_groups=mesh['yh'=4,'c'=2,'zh'=4,'zl'=2,'xh'=4,'xl'=2,'yl'=2] {'yh','zh','xh'}, dimensions={0} | all-to-all | bytes 262144 | tf_op jit(solution)/shard_map/all_to_all | solution.py:52
  98.0 0.1 broadcast_in_dim.7
  98.2 15.0 %all_to_all.23 = bf16[8,512,128]{2,1,0:T(8,128)(2,1)} all-to-all(bf16[8,512,128]{2,1,0:T(8,128)(2,1)S(1)} %broadcast_in_dim.7), channel_id=1, replica_groups=mesh['yh'=4,'c'=2,'zh'=4,'zl'=2,'xh'=4,'xl'=2,'yl'=2] {'zl','xl','yl'}, dimensions={0} | all-to-all | bytes 2097152 | tf_op jit(solution)/shard_map/all_to_all | solution.py:54
  113.2 6.7 %collective-permute-start.1 = (bf16[8,512,128]{2,1,0:T(8,128)(2,1)}, bf16[8,512,128]{2,1,0:T(8,128)(2,1)}, u32[]{:S(2)}, u32[]{:S(2)}) collective-permute-start(bf16[8,512,128]{2,1,0:T(8,128)(2,1)} %all_to_all.23), channel_id=1, source_target_pairs={{0,128},{128,0},{1,129},{129,1},{2,130},{130,2},{3,131},{131,3},{4... | collective-permute-start | bytes 3145736 | tf_op jit(solution)/shard_map/ppermute | solution.py:55
  119.9 1.8 %reshape.39 = bf16[64,4,2,1024]{3,2,1,0:T(2,128)(2,1)S(1)} reshape(bf16[64,8192]{1,0:T(8,128)(2,1)} %param.8) | data formatting | bytes 2097152 | tf_op jit(solution)/shard_map/reshape | solution.py:64
  121.8 2.7 %constant_dynamic-slice_fusion = (bf16[64,4,1,1024]{3,2,1,0:T(2,128)(2,1)S(1)}, bf16[64,4,1,1024]{3,2,1,0:T(2,128)(2,1)S(1)}) fusion(bf16[64,4,2,1024]{3,2,1,0:T(2,128)(2,1)S(1)} %reshape.39, s32[]{:T(128)S(6)} %select_n.11, s32[]{:T(128)S(6)} %select_n.10), kind=kLoop, calls=%fused_computation.15 | loop fusion | bytes 2097160 | tf_op jit(solution)/shard_map/jit(dynamic_index_in_dim)/dynamic_slice | solution.py:66
  124.5 1.5 %copy.19 = bf16[4,4,2,4,2,2,8,128]{7,6,5,4,3,2,1,0:T(8,128)(2,1)S(1)} copy(bf16[4,4,2,4,2,2,8,128]{7,6,3,1,0,5,4,2:T(8,128)(2,1)} %bitcast.10) | data formatting | bytes 2097152 | tf_op jit(solution)/shard_map/transpose | solution.py:61
  126.0 0.7 convolution_bitcast_fusion.1
  126.7 0.0 collective-permute-done.1
  126.7 1.5 %copy.21 = bf16[4,4,2,4,2,2,8,128]{7,6,5,4,3,2,1,0:T(8,128)(2,1)S(1)} copy(bf16[4,4,2,4,2,2,8,128]{7,6,3,1,0,5,4,2:T(8,128)(2,1)} %bitcast.15) | data formatting | bytes 2097152 | tf_op jit(solution)/shard_map/transpose | solution.py:61
  128.2 1.3 %fusion.2 = bf16[64,128]{1,0:T(8,128)(2,1)} fusion(f32[64,128]{1,0:T(8,128)S(1)} %convolution_bitcast_fusion.1, bf16[4,1024,128]{2,1,0:T(8,128)(2,1)S(1)} %bitcast.41, bf16[64,4,1,1024]{3,2,1,0:T(2,128)(2,1)S(1)} %get-tuple-element.8), kind=kOutput, calls=%fused_computation.6 | convolution fusion | flops 67125248 | bytes 1622016 | tf_op jit(solution)/shard_map/dot_general | solution.py:70
  (1 shorter events, 0.0 us)
Async XLA Ops:
  0.6 1.6 %copy-start = (bf16[128,8192]{1,0:T(8,128)(2,1)S(1)}, bf16[128,8192]{1,0:T(8,128)(2,1)}, u32[]{:S(2)}) copy-start(bf16[128,8192]{1,0:T(8,128)(2,1)} %param.6) | copy-start | bytes 6291460
  9.0 18.5 %collective-permute-start = (bf16[8,512,128]{2,1,0:T(8,128)(2,1)}, bf16[8,512,128]{2,1,0:T(8,128)(2,1)S(1)}, u32[]{:S(2)}, u32[]{:S(2)}) collective-permute-start(bf16[8,512,128]{2,1,0:T(8,128)(2,1)} %fusion.3), channel_id=1, source_target_pairs={{0,128},{128,0},{1,129},{129,1},{2,130},{130,2},{3,131},{131,3},{4... | collective-permute-start | bytes 3145736 | tf_op jit(solution)/shard_map/ppermute | solution.py:35
  29.3 48.5 %copy-start.1 = (f32[8,128]{1,0:T(8,128)S(1)}, f32[8,128]{1,0:T(8,128)}, u32[]{:S(2)}) copy-start(f32[8,128]{1,0:T(8,128)} %param.9) | copy-start | bytes 12292
  29.3 48.5 %copy-start.2 = (f32[8,128]{1,0:T(8,128)S(1)}, f32[8,128]{1,0:T(8,128)}, u32[]{:S(2)}) copy-start(f32[8,128]{1,0:T(8,128)} %param.10) | copy-start | bytes 12292
  29.3 48.5 %copy-start.3 = (f32[8,128]{1,0:T(8,128)S(1)}, f32[8,128]{1,0:T(8,128)}, u32[]{:S(2)}) copy-start(f32[8,128]{1,0:T(8,128)} %param.11) | copy-start | bytes 12292
  113.2 13.5 %collective-permute-start.1 = (bf16[8,512,128]{2,1,0:T(8,128)(2,1)}, bf16[8,512,128]{2,1,0:T(8,128)(2,1)}, u32[]{:S(2)}, u32[]{:S(2)}) collective-permute-start(bf16[8,512,128]{2,1,0:T(8,128)(2,1)} %all_to_all.23), channel_id=1, source_target_pairs={{0,128},{128,0},{1,129},{129,1},{2,130},{130,2},{3,131},{131,3},{4... | collective-permute-start | bytes 3145736 | tf_op jit(solution)/shard_map/ppermute | solution.py:55

commit v2 on v1

v2 whole, which is shorter than its diff:
```python
import functools

import jax
import jax.numpy as jnp
from jax import lax
from jax.experimental import pallas as pl
from jax.experimental.pallas import tpu as pltpu
from jax.sharding import Mesh, PartitionSpec as P

beta_one = 0.9
beta_two = 0.95
learn_rate = 0.003
decay_rate = 0.1
epsilon = 1e-08
steps_done = 10

AXES = ("yf", "ym", "c", "zf", "zm", "zl", "xf", "xm", "xl", "yl")
NEAR = ("zl", "xl", "yl")
MID = ("ym", "zm", "xm")
FAR = ("yf", "zf", "xf")
SWAP = [(0, 1), (1, 0)]
INTERPRET = False


def place(z, x):
    return (z % 2) * 2 + x % 2, (z // 2) * 2 + x // 2


def gradient_body(half_ref, tokens_ref, cotangent_ref, out_ref):
    cot = cotangent_ref[...]
    for z in range(4):
        for zl in range(2):
            at = (z * 2 + zl) * 128
            part = lax.dot_general(
                tokens_ref[:, at : at + 128], cot, (((0,), (0,)), ((), ())),
                preferred_element_type=jnp.float32,
            ).astype(out_ref.dtype)
            for block in range(16):
                x, low = block // 4, block % 4
                mid, far = place(z, x)
                out_ref[zl * 4 + low, 0, mid, 0, far] = part[block * 8 : block * 8 + 8]


def half_gradient(half, tokens_in, cotangent, dtype):
    return pl.pallas_call(
        gradient_body,
        out_shape=jax.ShapeDtypeStruct((8, 2, 4, 2, 4, 8, 128), dtype),
        grid_spec=pltpu.PrefetchScalarGridSpec(
            num_scalar_prefetch=1,
            grid=(4,),
            in_specs=[
                pl.BlockSpec((128, 1024), lambda i, half: (0, i * 2 + half[0])),
                pl.BlockSpec((128, 128), lambda i, half: (0, 0)),
            ],
            out_specs=pl.BlockSpec(
                (8, 1, 4, 1, 4, 8, 128), lambda i, half: (0, i % 2, 0, i // 2, 0, 0, 0)
            ),
        ),
        interpret=INTERPRET,
    )(half, tokens_in, cotangent)


def forward_body(half_ref, tokens_ref, weight_ref, start_ref, out_ref, total_ref):
    step = pl.program_id(0)

    @pl.when(step == 0)
    def _():
        total_ref[...] = start_ref[...]

    total = total_ref[...]
    for z in range(4):
        rows = []
        for zl in range(2):
            for block in range(16):
                x, low = block // 4, block % 4
                mid, far = place(z, x)
                rows.append(weight_ref[zl * 4 + low, 0, mid, 0, far].astype(jnp.float32))
        weight = jnp.concatenate(rows, axis=0).astype(jnp.bfloat16)
        total += jnp.dot(
            tokens_ref[:, z * 256 : z * 256 + 256], weight, preferred_element_type=jnp.float32
        )
    total_ref[...] = total
    out_ref[...] = total.astype(out_ref.dtype)


def half_forward(half, next_tokens, weight, start, dtype):
    rows = next_tokens.shape[0]
    return pl.pallas_call(
        forward_body,
        out_shape=jax.ShapeDtypeStruct((rows, 128), dtype),
        grid_spec=pltpu.PrefetchScalarGridSpec(
            num_scalar_prefetch=1,
            grid=(4,),
            in_specs=[
                pl.BlockSpec((rows, 1024), lambda i, half: (0, i * 2 + half[0])),
                pl.BlockSpec(
                    (8, 1, 4, 1, 4, 8, 128), lambda i, half: (0, i % 2, 0, i // 2, 0, 0, 0)
                ),
                pl.BlockSpec((rows, 128), lambda i, half: (0, 0)),
            ],
            out_specs=pl.BlockSpec((rows, 128), lambda i, half: (0, 0)),
            scratch_shapes=[pltpu.VMEM((rows, 128), jnp.float32)],
        ),
        interpret=INTERPRET,
    )(half, next_tokens, weight, start)


def exchange(value, axes):
    return lax.all_to_all(value, axes, 0, 0, tiled=True)


def summed(value):
    return jnp.sum(value.astype(jnp.float32), axis=0)


def on_device(tokens_in, cotangent, next_tokens, master, first_moment, second_moment):
    core = lax.axis_index("c")
    mine = core.reshape(1).astype(jnp.int32)
    theirs = 1 - mine
    bf16 = jnp.bfloat16

    give = half_gradient(theirs, tokens_in, cotangent, bf16)
    got = lax.ppermute(give, "c", SWAP)
    keep = half_gradient(mine, tokens_in, cotangent, jnp.float32)
    pair = (keep + got.astype(jnp.float32)).astype(bf16)
    near = summed(exchange(pair.reshape(8, 512, 128), NEAR)).astype(bf16)
    mid = summed(exchange(near.reshape(8, 64, 128), MID)).astype(bf16)
    gradient = summed(exchange(mid.reshape(8, 8, 128), FAR))

    new_first = beta_one * first_moment + (1.0 - beta_one) * gradient
    new_second = beta_two * second_moment + (1.0 - beta_two) * gradient * gradient
    first_hat = new_first / (1.0 - beta_one**steps_done)
    second_hat = new_second / (1.0 - beta_two**steps_done)
    new_master = master - learn_rate * (
        first_hat / (jnp.sqrt(second_hat) + epsilon) + decay_rate * master
    )
    low_weight = new_master.astype(bf16)

    far = exchange(jnp.broadcast_to(low_weight, (8, 8, 128)), FAR).reshape(64, 128)
    mid = exchange(jnp.broadcast_to(far, (8, 64, 128)), MID).reshape(512, 128)
    near = exchange(jnp.broadcast_to(mid, (8, 512, 128)), NEAR)
    near = near.reshape(8, 2, 4, 2, 4, 8, 128)
    other = lax.ppermute(near, "c", SWAP)
    rows = next_tokens.shape[0]
    start = jnp.zeros((rows, 128), jnp.float32)
    own_part = half_forward(mine, next_tokens, near, start, jnp.float32)
    next_out = half_forward(theirs, next_tokens, other, own_part, bf16)
    return (new_master, new_first, new_second, next_out)


def solution(mesh):
    fine = Mesh(mesh.devices.reshape(2, 2, 2, 2, 2, 2, 2, 2, 2, 2), AXES)
    spec = P(AXES, None)
    return jax.shard_map(
        on_device, mesh=fine, in_specs=(spec,) * 6, out_specs=(spec,) * 4, check_vma=False
    )
```

time: 130 us -> 148 us (1.14)
  blocking collectives: 82.9 us -> 102 us
  Pallas kernels: 0 us -> 14.8 us
  local copies, waits for them, and re-layouts: 14.6 us -> 1.78 us
  matrix products: 3.55 us -> 0 us
  waiting for transfers between devices: 2.48 us -> 0.01 us
  starting transfers between devices: 22.7 us -> 24.9 us
    all_to_all x4 -> x6, blocking collectives: 82.9 us -> 102 us  [exchange(): return lax.all_to_all(value, axes, 0, 0, tiled=True)]
    pallas_call x0 -> x4, Pallas kernels: none -> 14.8 us  [the longest x2 8.15 us: half_gradient(): pl.pallas_call(gradient_body, out_shape=jax.ShapeDtypeStruct((8, 2, 4, 2,...]
    reshape x2 -> x0, local copies, waits for them, and re-layouts: 4.36 us -> none  [the longest x1 2.53 us: on_device(): gradient.reshape(*sizes, own_rows, cols)]
    dot_general x3 -> x0, matrix products: 3.55 us -> none  [the longest x1 1.51 us: on_device(): lax.dot_general(tokens_in, cotangent, (((0,), (0,)), ((), ())), preferred...]
    transpose x2 -> x0, local copies, waits for them, and re-layouts: 2.99 us -> none  [natural(): half = half.transpose(3, 4, 0, 5, 1, 2, 6, 7)]
    dynamic_slice x1 -> x0, local copies, waits for them, and re-layouts: 2.74 us -> none  [on_device(): other_tokens = lax.dynamic_index_in_dim(tokens, 1 - core, 2, keepdims=False)]
    convert_element_type x1 -> x0, local copies, waits for them, and re-layouts: 2.74 us -> none  [on_device(): got = lax.ppermute(give.astype(jnp.bfloat16), 'c', swap)]
    ppermute x2, waiting for transfers between devices: 2.48 us -> 0.01 us  [the longest x1 0.01 us: on_device(): got = lax.ppermute(give, 'c', SWAP)]
  transfers between devices with their start and end apart: 2 -> 2, of which waited for: 1 -> 0; matrix products, arithmetic and copies ran while one was open for 5% -> 0% of each run, Pallas kernels for 0% -> 5%
where the time goes in v2:
time: 148 us; the launch traced here: 147 us
  blocking collectives  102 us (69%)
  starting transfers between devices  24.9 us (17%)
  Pallas kernels  14.8 us (10%)
  other arithmetic  2.78 us (2%)
  local copies, waits for them, and re-layouts  1.78 us (1%)
    all_to_all x6, blocking collectives, exchange(): return lax.all_to_all(value, axes, 0, 0, tiled=True)  102 us
    ppermute x1, starting transfers between devices, on_device(): got = lax.ppermute(give, 'c', SWAP)  16 us
    ppermute x1, starting transfers between devices, on_device(): other = lax.ppermute(near, 'c', SWAP)  8.92 us
    pallas_call x2, Pallas kernels, half_gradient(): pl.pallas_call(gradient_body, out_shape=jax.ShapeDtypeStruct((8, 2, 4, 2,...  8.15 us
    pallas_call x2, Pallas kernels, half_forward(): pl.pallas_call(forward_body, out_shape=jax.ShapeDtypeStruct((rows, 128),...  6.63 us
  transfers between devices with their start and end apart: 2, of which 0 were waited for; matrix products, arithmetic and copies ran while one was open for 0% of the time, Pallas kernels for 5%

profile of v2, /device:TPU:1, one launch (start us, length us, event | category | flops | bytes accessed | tf_op | source)
XLA Modules:
  0.0 147.1 jit_solution(13216561897527538080)
XLA Ops:
  0.6 4.0 %shard_map.94 = bf16[8,2,4,2,4,8,128]{6,5,4,3,2,1,0:T(8,128)(2,1)} custom-call(s32[1]{0:T(128)S(6)} %sub.6.half_ref, bf16[128,8192]{1,0:T(8,128)(2,1)} %tokens_ref.5, bf16[128,128]{1,0:T(8,128)(2,1)} %cotangent_ref.3), custom_call_target="tpu_custom_call" | custom-call | tf_op jit(solution)/shard_map/pallas_call | solution.py:45
  4.6 16.0 %collective-permute-start = (bf16[8,2,4,2,4,8,128]{6,5,4,3,2,1,0:T(8,128)(2,1)}, bf16[8,2,4,2,4,8,128]{6,5,4,3,2,1,0:T(8,128)(2,1)S(1)}, u32[]{:S(2)}, u32[]{:S(2)}) collective-permute-start(bf16[8,2,4,2,4,8,128]{6,5,4,3,2,1,0:T(8,128)(2,1)} %shard_map.94), channel_id=1, source_target_pairs={{0,128},{128,0},{1,129},{129,1},{2,130},{130,2},{3,131},{131,3},{4... | collective-permute-start | bytes 3145736 | tf_op jit(solution)/shard_map/ppermute | solution.py:123
  20.6 4.2 %shard_map.93 = f32[8,2,4,2,4,8,128]{6,5,4,3,2,1,0:T(8,128)} custom-call(s32[1]{0:T(128)} %bitcast.half_ref, bf16[128,8192]{1,0:T(8,128)(2,1)} %tokens_ref.5, bf16[128,128]{1,0:T(8,128)(2,1)} %cotangent_ref.3), custom_call_target="tpu_custom_call" | custom-call | tf_op jit(solution)/shard_map/pallas_call | solution.py:45
  24.8 0.0 collective-permute-done
  24.8 2.0 %add_convert_fusion = bf16[8,2,4,2,4,8,128]{6,5,4,3,2,1,0:T(8,128)(2,1)S(1)} fusion(f32[8,2,4,2,4,8,128]{6,5,4,3,2,1,0:T(8,128)} %shard_map.93, bf16[8,2,4,2,4,8,128]{6,5,4,3,2,1,0:T(8,128)(2,1)S(1)} %collective-permute-done), kind=kLoop, calls=%fused_computation | loop fusion | flops 1572864 | bytes 4194304 | tf_op jit(solution)/shard_map/convert_element_type | solution.py:125
  26.8 0.0 copy-start.2
  26.8 0.0 copy-start.3
  26.8 0.0 copy-start.4
  26.8 17.7 %all_to_all.30 = bf16[8,512,128]{2,1,0:T(8,128)(2,1)S(1)} all-to-all(bf16[8,512,128]{2,1,0:T(8,128)(2,1)S(1)} %bitcast.9), channel_id=1, replica_groups=mesh['yf'=2,'ym'=2,'c'=2,'zf'=2,'zm'=2,'zl'=2,'xf'=2,'xm'=2,'xl'=2,'yl'=..., dimensions={0} | all-to-all | bytes 2097152 | tf_op jit(solution)/shard_map/all_to_all | solution.py:109
  44.6 0.1 reduce_sum.33
  44.7 10.6 %all_to_all.31 = bf16[8,64,128]{2,1,0:T(8,128)(2,1)S(1)} all-to-all(bf16[8,64,128]{2,1,0:T(8,128)(2,1)S(1)} %bitcast.10), channel_id=1, replica_groups=mesh['yf'=2,'ym'=2,'c'=2,'zf'=2,'zm'=2,'zl'=2,'xf'=2,'xm'=2,'xl'=2,'yl'=..., dimensions={0} | all-to-all | bytes 262144 | tf_op jit(solution)/shard_map/all_to_all | solution.py:109
  55.3 31.4 %all_to_all.32 = bf16[8,8,128]{2,1,0:T(8,128)(2,1)S(1)} all-to-all(bf16[8,8,128]{2,1,0:T(8,128)(2,1)S(1)} %bitcast.12), channel_id=1, replica_groups=mesh['yf'=2,'ym'=2,'c'=2,'zf'=2,'zm'=2,'zl'=2,'xf'=2,'xm'=2,'xl'=2,'yl'=..., dimensions={0} | all-to-all | bytes 32768 | tf_op jit(solution)/shard_map/all_to_all | solution.py:109
  86.7 0.0 copy-done.2
  86.7 0.0 copy-done.3
  86.7 0.0 copy-done.4
  86.7 0.6 fusion.1
  87.4 18.6 %all_to_all.33 = bf16[8,8,128]{2,1,0:T(8,128)(2,1)S(1)} all-to-all(bf16[8,8,128]{2,1,0:T(8,128)(2,1)S(1)} %broadcast_in_dim.12), channel_id=1, replica_groups=mesh['yf'=2,'ym'=2,'c'=2,'zf'=2,'zm'=2,'zl'=2,'xf'=2,'xm'=2,'xl'=2,'yl'=..., dimensions={0} | all-to-all | bytes 32768 | tf_op jit(solution)/shard_map/all_to_all | solution.py:109
  106.0 10.2 %all_to_all.34 = bf16[8,64,128]{2,1,0:T(8,128)(2,1)S(1)} all-to-all(bf16[8,64,128]{2,1,0:T(8,128)(2,1)S(1)} %broadcast_in_dim.13), channel_id=1, replica_groups=mesh['yf'=2,'ym'=2,'c'=2,'zf'=2,'zm'=2,'zl'=2,'xf'=2,'xm'=2,'xl'=2,'yl'=..., dimensions={0} | all-to-all | bytes 262144 | tf_op jit(solution)/shard_map/all_to_all | solution.py:109
  116.2 0.1 broadcast_in_dim.14
  116.3 13.6 %all_to_all.35 = bf16[8,512,128]{2,1,0:T(8,128)(2,1)S(1)} all-to-all(bf16[8,512,128]{2,1,0:T(8,128)(2,1)S(1)} %broadcast_in_dim.14), channel_id=1, replica_groups=mesh['yf'=2,'ym'=2,'c'=2,'zf'=2,'zm'=2,'zl'=2,'xf'=2,'xm'=2,'xl'=2,'yl'=..., dimensions={0} | all-to-all | bytes 2097152 | tf_op jit(solution)/shard_map/all_to_all | solution.py:109
  129.9 0.0 copy-start
  129.9 8.9 %collective-permute-start.1 = (bf16[8,2,4,2,4,8,128]{6,5,4,3,2,1,0:T(8,128)(2,1)S(1)}, bf16[8,2,4,2,4,8,128]{6,5,4,3,2,1,0:T(8,128)(2,1)S(1)}, u32[]{:S(2)}, u32[]{:S(2)}) collective-permute-start(bf16[8,2,4,2,4,8,128]{6,5,4,3,2,1,0:T(8,128)(2,1)S(1)} %bitcast.7), channel_id=1, source_target_pairs={{0,128},{128,0},{1,129},{129,1},{2,130},{130,2},{3,131},{131,3},{4... | collective-permute-start | bytes 3145736 | tf_op jit(solution)/shard_map/ppermute | solution.py:143
  138.9 0.6 broadcast_in_dim.15.start_ref
  139.5 0.0 copy-done
  139.5 3.3 %shard_map.95.start_ref = f32[64,128]{1,0:T(8,128)} custom-call(s32[1]{0:T(128)} %bitcast.half_ref, bf16[64,8192]{1,0:T(8,128)(2,1)} %tokens_ref.7, bf16[8,2,4,2,4,8,128]{6,5,4,3,2,1,0:T(8,128)(2,1)} %bitcast.8, f32[64,128]{1,0:T(8,128)} %broadcast_in_dim.15.start_ref), custom_call_target="tpu_custom_call" | custom-call | tf_op jit(solution)/shard_map/pallas_call | solution.py:88
  142.8 0.0 collective-permute-done.1.weight_ref
  142.8 0.0 copy-start.1
  142.8 1.0 copy-done.1
  143.8 3.3 %shard_map.96 = bf16[64,128]{1,0:T(8,128)(2,1)} custom-call(s32[1]{0:T(128)S(6)} %sub.6.half_ref, bf16[64,8192]{1,0:T(8,128)(2,1)} %tokens_ref.7, bf16[8,2,4,2,4,8,128]{6,5,4,3,2,1,0:T(8,128)(2,1)} %copy-done.1, f32[64,128]{1,0:T(8,128)} %shard_map.95.start_ref), custom_call_target="tpu_custom_call" | custom-call | tf_op jit(solution)/shard_map/pallas_call | solution.py:88
  (4 shorter events, 0.1 us)
Async XLA Ops:
  4.6 20.2 %collective-permute-start = (bf16[8,2,4,2,4,8,128]{6,5,4,3,2,1,0:T(8,128)(2,1)}, bf16[8,2,4,2,4,8,128]{6,5,4,3,2,1,0:T(8,128)(2,1)S(1)}, u32[]{:S(2)}, u32[]{:S(2)}) collective-permute-start(bf16[8,2,4,2,4,8,128]{6,5,4,3,2,1,0:T(8,128)(2,1)} %shard_map.94), channel_id=1, source_target_pairs={{0,128},{128,0},{1,129},{129,1},{2,130},{130,2},{3,131},{131,3},{4... | collective-permute-start | bytes 3145736 | tf_op jit(solution)/shard_map/ppermute | solution.py:123
  26.8 59.9 %copy-start.2 = (f32[8,128]{1,0:T(8,128)S(1)}, f32[8,128]{1,0:T(8,128)}, u32[]{:S(2)}) copy-start(f32[8,128]{1,0:T(8,128)} %param.9) | copy-start | bytes 12292
  26.8 59.9 %copy-start.3 = (f32[8,128]{1,0:T(8,128)S(1)}, f32[8,128]{1,0:T(8,128)}, u32[]{:S(2)}) copy-start(f32[8,128]{1,0:T(8,128)} %param.10) | copy-start | bytes 12292
  26.8 59.9 %copy-start.4 = (f32[8,128]{1,0:T(8,128)S(1)}, f32[8,128]{1,0:T(8,128)}, u32[]{:S(2)}) copy-start(f32[8,128]{1,0:T(8,128)} %param.11) | copy-start | bytes 12292
  129.9 9.5 %copy-start = (bf16[8,512,128]{2,1,0:T(8,128)(2,1)}, bf16[8,512,128]{2,1,0:T(8,128)(2,1)S(1)}, u32[]{:S(2)}) copy-start(bf16[8,512,128]{2,1,0:T(8,128)(2,1)S(1)} %all_to_all.35) | copy-start | bytes 3145732
  129.9 12.9 %collective-permute-start.1 = (bf16[8,2,4,2,4,8,128]{6,5,4,3,2,1,0:T(8,128)(2,1)S(1)}, bf16[8,2,4,2,4,8,128]{6,5,4,3,2,1,0:T(8,128)(2,1)S(1)}, u32[]{:S(2)}, u32[]{:S(2)}) collective-permute-start(bf16[8,2,4,2,4,8,128]{6,5,4,3,2,1,0:T(8,128)(2,1)S(1)} %bitcast.7), channel_id=1, source_target_pairs={{0,128},{128,0},{1,129},{129,1},{2,130},{130,2},{3,131},{131,3},{4... | collective-permute-start | bytes 3145736 | tf_op jit(solution)/shard_map/ppermute | solution.py:143
  142.8 1.0 copy-start.1

commit v3 on v1

v3 whole, which is shorter than its diff:
```python
import jax
import jax.numpy as jnp
from jax import lax
from jax.experimental import pallas as pl
from jax.experimental.pallas import tpu as pltpu
from jax.sharding import Mesh, PartitionSpec as P

beta_one = 0.9
beta_two = 0.95
learn_rate = 0.003
decay_rate = 0.1
epsilon = 1e-08
steps_done = 10

AXES = ("yh", "c", "zh", "zl", "xh", "xl", "yl")
NEAR = ("zl", "xl", "yl")
FAR = ("yh", "zh", "xh")
SWAP = [(0, 1), (1, 0)]
INTERPRET = False
SMEM = pl.BlockSpec(memory_space=pltpu.SMEM)
VMEM = pl.BlockSpec(memory_space=pltpu.VMEM)


def held(array):
    return array if INTERPRET else pltpu.with_memory_space_constraint(array, pltpu.VMEM)


def in_vmem(shape, dtype):
    return (jax.ShapeDtypeStruct if INTERPRET else pltpu.VMEM)(shape, dtype)


def blocks(half):
    for y in range(4):
        for z in range(4):
            for zl in range(2):
                start = pl.multiple_of(y * 2048 + half * 1024 + (z * 2 + zl) * 128, 128)
                for block in range(16):
                    x, low = block // 4, block % 4
                    yield start + block * 8, (zl * 4 + low, y, z * 4 + x)


def give_body(half_ref, gradient_ref, out_ref):
    for row, place in blocks(half_ref[0]):
        out_ref[place] = gradient_ref[pl.ds(row, 8), :].astype(out_ref.dtype)


def pair_body(half_ref, gradient_ref, got_ref, out_ref):
    for row, place in blocks(half_ref[0]):
        both = gradient_ref[pl.ds(row, 8), :] + got_ref[place].astype(jnp.float32)
        out_ref[place] = both.astype(out_ref.dtype)


def rearranged(body, half, *arrays):
    return pl.pallas_call(
        body,
        out_shape=in_vmem((8, 4, 16, 8, 128), jnp.bfloat16),
        in_specs=[SMEM] + [VMEM] * len(arrays),
        out_specs=VMEM,
        compiler_params=pltpu.CompilerParams(vmem_limit_bytes=16 << 20),
        interpret=INTERPRET,
    )(half, *[held(a) for a in arrays])


def forward_body(half_ref, tokens_ref, weight_ref, start_ref, out_ref):
    total = None if start_ref is None else start_ref[...]
    for y in range(4):
        for z in range(4):
            rows = []
            for zl in range(2):
                for block in range(16):
                    x, low = block // 4, block % 4
                    rows.append(weight_ref[zl * 4 + low, y, z * 4 + x].astype(jnp.float32))
            weight = jnp.concatenate(rows, axis=0).astype(jnp.bfloat16)
            at = pl.multiple_of(y * 2048 + half_ref[0] * 1024 + z * 256, 256)
            part = jnp.dot(
                tokens_ref[:, pl.ds(at, 256)], weight, preferred_element_type=jnp.float32
            )
            total = part if total is None else total + part
    out_ref[...] = total.astype(out_ref.dtype)


def first_body(half_ref, tokens_ref, weight_ref, out_ref):
    forward_body(half_ref, tokens_ref, weight_ref, None, out_ref)


def half_forward(half, next_tokens, weight, start, dtype):
    arrays = (next_tokens, weight) if start is None else (next_tokens, weight, start)
    return pl.pallas_call(
        first_body if start is None else forward_body,
        out_shape=(in_vmem if start is None else jax.ShapeDtypeStruct)(
            (next_tokens.shape[0], 128), dtype
        ),
        in_specs=[SMEM] + [VMEM] * len(arrays),
        out_specs=VMEM,
        compiler_params=pltpu.CompilerParams(vmem_limit_bytes=16 << 20),
        interpret=INTERPRET,
    )(half, *[held(a) for a in arrays])


def exchange(value, axes):
    return lax.all_to_all(value, axes, 0, 0, tiled=True)


def summed(value):
    return jnp.sum(value.astype(jnp.float32), axis=0)


def on_device(tokens_in, cotangent, next_tokens, master, first_moment, second_moment):
    core = lax.axis_index("c")
    mine = core.reshape(1).astype(jnp.int32)
    theirs = 1 - mine
    bf16 = jnp.bfloat16

    local = lax.dot_general(
        tokens_in, cotangent, (((0,), (0,)), ((), ())), preferred_element_type=jnp.float32
    )
    give = rearranged(give_body, theirs, local)
    got = lax.ppermute(give, "c", SWAP)
    pair = rearranged(pair_body, mine, local, got)
    near = summed(exchange(pair.reshape(8, 512, 128), NEAR)).astype(bf16)
    gradient = summed(exchange(near.reshape(64, 8, 128), FAR))

    new_first = beta_one * first_moment + (1.0 - beta_one) * gradient
    new_second = beta_two * second_moment + (1.0 - beta_two) * gradient * gradient
    first_hat = new_first / (1.0 - beta_one**steps_done)
    second_hat = new_second / (1.0 - beta_two**steps_done)
    new_master = master - learn_rate * (
        first_hat / (jnp.sqrt(second_hat) + epsilon) + decay_rate * master
    )
    low_weight = new_master.astype(bf16)

    far = exchange(jnp.broadcast_to(low_weight, (64, 8, 128)), FAR).reshape(512, 128)
    near = exchange(jnp.broadcast_to(far, (8, 512, 128)), NEAR)
    near = near.reshape(8, 4, 16, 8, 128)
    other = lax.ppermute(near, "c", SWAP)
    own_part = half_forward(mine, next_tokens, near, None, jnp.float32)
    next_out = half_forward(theirs, next_tokens, other, own_part, bf16)
    return (new_master, new_first, new_second, next_out)


def solution(mesh):
    fine = Mesh(mesh.devices.reshape(4, 2, 4, 2, 4, 2, 2), AXES)
    spec = P(AXES, None)
    return jax.shard_map(
        on_device, mesh=fine, in_specs=(spec,) * 6, out_specs=(spec,) * 4, check_vma=False
    )
```

time: 130 us -> 117 us (0.900)
  local copies, waits for them, and re-layouts: 14.6 us -> 1.76 us
  matrix products: 3.55 us -> 1.51 us
  other arithmetic: 2.64 us -> 0.84 us
  waiting for transfers between devices: 2.48 us -> 4.21 us
  Pallas kernels: 0 us -> 1.62 us
    reshape x2 -> x0, local copies, waits for them, and re-layouts: 4.36 us -> none  [the longest x1 2.53 us: on_device(): gradient.reshape(*sizes, own_rows, cols)]
    transpose x2 -> x0, local copies, waits for them, and re-layouts: 2.99 us -> none  [natural(): half = half.transpose(3, 4, 0, 5, 1, 2, 6, 7)]
    dynamic_slice x1 -> x0, local copies, waits for them, and re-layouts: 2.74 us -> none  [on_device(): other_tokens = lax.dynamic_index_in_dim(tokens, 1 - core, 2, keepdims=False)]
    convert_element_type x1 -> x0, local copies, waits for them, and re-layouts: 2.74 us -> none  [on_device(): got = lax.ppermute(give.astype(jnp.bfloat16), 'c', swap)]
    dot_general x2 -> x0, matrix products: 2.05 us -> none  [the longest x1 1.33 us: on_device(): lax.dot_general(other_tokens, natural(other), contract, preferred_element...]
    convert_element_type x2 -> x1, other arithmetic: 2.43 us -> 0.62 us  [on_device(): low_weight = new_master.astype(bf16)]
    ppermute x2, waiting for transfers between devices: 2.48 us -> 4.21 us  [the longest x1 2.26 us: on_device(): got = lax.ppermute(give, 'c', SWAP)]
    pallas_call x0 -> x4, Pallas kernels: none -> 1.62 us  [the longest x2 1.22 us: half_forward(): pl.pallas_call(first_body if start is None else forward_body, out_shape=(...]
  transfers between devices with their start and end apart: 2 -> 2, of which waited for: 1 -> 2; matrix products, arithmetic and copies ran while one was open for 5% -> 0% of each run, Pallas kernels for 0% -> 0%
where the time goes in v3:
time: 117 us; the launch traced here: 116 us
  blocking collectives  83.4 us (71%)
  starting transfers between devices  22.1 us (19%)
  waiting for transfers between devices  4.21 us (4%)
  local copies, waits for them, and re-layouts  1.76 us (2%)
  Pallas kernels  1.62 us (1%)
  matrix products  1.51 us (1%)
    all_to_all x4, blocking collectives, exchange(): return lax.all_to_all(value, axes, 0, 0, tiled=True)  83.4 us
    ppermute x1, starting transfers between devices, on_device(): got = lax.ppermute(give, 'c', SWAP)  16 us
    ppermute x1, starting transfers between devices, on_device(): other = lax.ppermute(near, 'c', SWAP)  6.12 us
  transfers between devices with their start and end apart: 2, of which 2 were waited for; matrix products, arithmetic and copies ran while one was open for 0% of the time, Pallas kernels for 0%

profile of v3, /device:TPU:1, one launch (start us, length us, event | category | flops | bytes accessed | tf_op | source)
XLA Modules:
  0.0 116.2 jit_solution(17409316472411774941)
XLA Ops:
  0.6 0.0 copy-start
  0.7 1.6 %copy-done = bf16[128,8192]{1,0:T(8,128)(2,1)S(1)} copy-done((bf16[128,8192]{1,0:T(8,128)(2,1)S(1)}, bf16[128,8192]{1,0:T(8,128)(2,1)}, u32[]{:S(2)}) %copy-start) | copy-done | bytes 2097176
  2.2 1.5 %fusion.3.gradient_ref = f32[8192,128]{1,0:T(8,128)S(1)} fusion(bf16[128,8192]{1,0:T(8,128)(2,1)S(1)} %copy-done, bf16[128,128]{1,0:T(8,128)(2,1)} %param.7), kind=kOutput, calls=%fused_computation.6 | convolution fusion | flops 268435456 | bytes 6324224 | tf_op jit(solution)/shard_map/dot_general | solution.py:114
  3.7 0.1 shard_map.93
  3.9 16.0 %collective-permute-start = (bf16[8,4,16,8,128]{4,3,2,1,0:T(8,128)(2,1)S(1)}, bf16[8,4,16,8,128]{4,3,2,1,0:T(8,128)(2,1)S(1)}, u32[]{:S(2)}, u32[]{:S(2)}) collective-permute-start(bf16[8,4,16,8,128]{4,3,2,1,0:T(8,128)(2,1)S(1)} %shard_map.93), channel_id=1, source_target_pairs={{0,128},{128,0},{1,129},{129,1},{2,130},{130,2},{3,131},{131,3},{4... | collective-permute-start | bytes 3145736 | tf_op jit(solution)/shard_map/ppermute | solution.py:118
  19.9 2.3 %collective-permute-done.got_ref = bf16[8,4,16,8,128]{4,3,2,1,0:T(8,128)(2,1)S(1)} collective-permute-done((bf16[8,4,16,8,128]{4,3,2,1,0:T(8,128)(2,1)S(1)}, bf16[8,4,16,8,128]{4,3,2,1,0:T(8,128)(2,1)S(1)}, u32[]{:S(2)}, u32[]{:S(2)}) %collective-permute-start) | collective-permute-done | bytes 1048608 | tf_op jit(solution)/shard_map/ppermute | solution.py:118
  22.2 0.3 shard_map.94
  22.4 0.0 copy-start.2
  22.5 0.0 copy-start.3
  22.5 0.0 copy-start.4
  22.5 17.5 %all_to_all.20 = bf16[8,512,128]{2,1,0:T(8,128)(2,1)S(1)} all-to-all(bf16[8,512,128]{2,1,0:T(8,128)(2,1)S(1)} %bitcast.7), channel_id=1, replica_groups=mesh['yh'=4,'c'=2,'zh'=4,'zl'=2,'xh'=4,'xl'=2,'yl'=2] {'zl','xl','yl'}, dimensions={0} | all-to-all | bytes 2097152 | tf_op jit(solution)/shard_map/all_to_all | solution.py:101
  40.0 0.1 reduce_sum.21
  40.1 0.0 copy-start.1
  40.2 30.9 %all_to_all.21 = bf16[64,8,128]{2,1,0:T(8,128)(2,1)S(1)} all-to-all(bf16[64,8,128]{2,1,0:T(8,128)(2,1)S(1)} %bitcast.10), channel_id=1, replica_groups=mesh['yh'=4,'c'=2,'zh'=4,'zl'=2,'xh'=4,'xl'=2,'yl'=2] {'yh','zh','xh'}, dimensions={0} | all-to-all | bytes 262144 | tf_op jit(solution)/shard_map/all_to_all | solution.py:101
  71.1 0.1 convert_reduce_fusion
  71.1 0.0 copy-done.2
  71.1 0.0 copy-done.3
  71.1 0.0 copy-done.4
  71.2 0.6 fusion.1
  71.8 19.5 %all_to_all.22 = bf16[64,8,128]{2,1,0:T(8,128)(2,1)S(1)} all-to-all(bf16[64,8,128]{2,1,0:T(8,128)(2,1)S(1)} %broadcast_in_dim.6), channel_id=1, replica_groups=mesh['yh'=4,'c'=2,'zh'=4,'zl'=2,'xh'=4,'xl'=2,'yl'=2] {'yh','zh','xh'}, dimensions={0} | all-to-all | bytes 262144 | tf_op jit(solution)/shard_map/all_to_all | solution.py:101
  91.3 0.1 broadcast_in_dim.7
  91.5 15.5 %all_to_all.23 = bf16[8,512,128]{2,1,0:T(8,128)(2,1)S(1)} all-to-all(bf16[8,512,128]{2,1,0:T(8,128)(2,1)S(1)} %broadcast_in_dim.7), channel_id=1, replica_groups=mesh['yh'=4,'c'=2,'zh'=4,'zl'=2,'xh'=4,'xl'=2,'yl'=2] {'zl','xl','yl'}, dimensions={0} | all-to-all | bytes 2097152 | tf_op jit(solution)/shard_map/all_to_all | solution.py:101
  106.9 6.1 %collective-permute-start.1 = (bf16[8,4,16,8,128]{4,3,2,1,0:T(8,128)(2,1)S(1)}, bf16[8,4,16,8,128]{4,3,2,1,0:T(8,128)(2,1)S(1)}, u32[]{:S(2)}, u32[]{:S(2)}) collective-permute-start(bf16[8,4,16,8,128]{4,3,2,1,0:T(8,128)(2,1)S(1)} %bitcast.8), channel_id=1, source_target_pairs={{0,128},{128,0},{1,129},{129,1},{2,130},{130,2},{3,131},{131,3},{4... | collective-permute-start | bytes 3145736 | tf_op jit(solution)/shard_map/ppermute | solution.py:135
  113.0 0.0 copy-done.1
  113.1 0.3 shard_map.95.start_ref
  113.4 1.9 %collective-permute-done.1.weight_ref = bf16[8,4,16,8,128]{4,3,2,1,0:T(8,128)(2,1)S(1)} collective-permute-done((bf16[8,4,16,8,128]{4,3,2,1,0:T(8,128)(2,1)S(1)}, bf16[8,4,16,8,128]{4,3,2,1,0:T(8,128)(2,1)S(1)}, u32[]{:S(2)}, u32[]{:S(2)}) %collective-permute-start.1) | collective-permute-done | bytes 1048608 | tf_op jit(solution)/shard_map/ppermute | solution.py:135
  115.3 0.9 shard_map.96
  (1 shorter events, 0.0 us)
Async XLA Ops:
  0.6 1.6 %copy-start = (bf16[128,8192]{1,0:T(8,128)(2,1)S(1)}, bf16[128,8192]{1,0:T(8,128)(2,1)}, u32[]{:S(2)}) copy-start(bf16[128,8192]{1,0:T(8,128)(2,1)} %param.6) | copy-start | bytes 6291460
  3.9 18.3 %collective-permute-start = (bf16[8,4,16,8,128]{4,3,2,1,0:T(8,128)(2,1)S(1)}, bf16[8,4,16,8,128]{4,3,2,1,0:T(8,128)(2,1)S(1)}, u32[]{:S(2)}, u32[]{:S(2)}) collective-permute-start(bf16[8,4,16,8,128]{4,3,2,1,0:T(8,128)(2,1)S(1)} %shard_map.93), channel_id=1, source_target_pairs={{0,128},{128,0},{1,129},{129,1},{2,130},{130,2},{3,131},{131,3},{4... | collective-permute-start | bytes 3145736 | tf_op jit(solution)/shard_map/ppermute | solution.py:118
  22.4 48.7 %copy-start.2 = (f32[8,128]{1,0:T(8,128)S(1)}, f32[8,128]{1,0:T(8,128)}, u32[]{:S(2)}) copy-start(f32[8,128]{1,0:T(8,128)} %param.9) | copy-start | bytes 12292
  22.5 48.7 %copy-start.3 = (f32[8,128]{1,0:T(8,128)S(1)}, f32[8,128]{1,0:T(8,128)}, u32[]{:S(2)}) copy-start(f32[8,128]{1,0:T(8,128)} %param.10) | copy-start | bytes 12292
  22.5 48.7 %copy-start.4 = (f32[8,128]{1,0:T(8,128)S(1)}, f32[8,128]{1,0:T(8,128)}, u32[]{:S(2)}) copy-start(f32[8,128]{1,0:T(8,128)} %param.11) | copy-start | bytes 12292
  40.1 72.9 %copy-start.1 = (bf16[64,8192]{1,0:T(8,128)(2,1)S(1)}, bf16[64,8192]{1,0:T(8,128)(2,1)}, u32[]{:S(2)}) copy-start(bf16[64,8192]{1,0:T(8,128)(2,1)} %tokens_ref.3) | copy-start | bytes 3145732
  106.9 8.4 %collective-permute-start.1 = (bf16[8,4,16,8,128]{4,3,2,1,0:T(8,128)(2,1)S(1)}, bf16[8,4,16,8,128]{4,3,2,1,0:T(8,128)(2,1)S(1)}, u32[]{:S(2)}, u32[]{:S(2)}) collective-permute-start(bf16[8,4,16,8,128]{4,3,2,1,0:T(8,128)(2,1)S(1)} %bitcast.8), channel_id=1, source_target_pairs={{0,128},{128,0},{1,129},{129,1},{2,130},{130,2},{3,131},{131,3},{4... | collective-permute-start | bytes 3145736 | tf_op jit(solution)/shard_map/ppermute | solution.py:135

commit v4 on v3

--- a/solution.py
+++ b/solution.py
@@ -61,8 +61,8 @@
     )(half, *[held(a) for a in arrays])
 
 
-def forward_body(half_ref, tokens_ref, weight_ref, start_ref, out_ref):
-    total = None if start_ref is None else start_ref[...]
+def forward_body(half_ref, tokens_ref, weight_ref, out_ref):
+    total = jnp.zeros(out_ref.shape, jnp.float32)
     for y in range(4):
         for z in range(4):
             rows = []
@@ -72,29 +72,21 @@
                     rows.append(weight_ref[zl * 4 + low, y, z * 4 + x].astype(jnp.float32))
             weight = jnp.concatenate(rows, axis=0).astype(jnp.bfloat16)
             at = pl.multiple_of(y * 2048 + half_ref[0] * 1024 + z * 256, 256)
-            part = jnp.dot(
+            total += jnp.dot(
                 tokens_ref[:, pl.ds(at, 256)], weight, preferred_element_type=jnp.float32
             )
-            total = part if total is None else total + part
-    out_ref[...] = total.astype(out_ref.dtype)
+    out_ref[...] = total
 
 
-def first_body(half_ref, tokens_ref, weight_ref, out_ref):
-    forward_body(half_ref, tokens_ref, weight_ref, None, out_ref)
-
-
-def half_forward(half, next_tokens, weight, start, dtype):
-    arrays = (next_tokens, weight) if start is None else (next_tokens, weight, start)
+def half_forward(half, next_tokens, weight):
     return pl.pallas_call(
-        first_body if start is None else forward_body,
-        out_shape=(in_vmem if start is None else jax.ShapeDtypeStruct)(
-            (next_tokens.shape[0], 128), dtype
-        ),
-        in_specs=[SMEM] + [VMEM] * len(arrays),
+        forward_body,
+        out_shape=in_vmem((next_tokens.shape[0], 128), jnp.float32),
+        in_specs=[SMEM, VMEM, VMEM],
         out_specs=VMEM,
         compiler_params=pltpu.CompilerParams(vmem_limit_bytes=16 << 20),
         interpret=INTERPRET,
-    )(half, *[held(a) for a in arrays])
+    )(half, held(next_tokens), held(weight))
 
 
 def exchange(value, axes):
@@ -111,6 +103,7 @@
     theirs = 1 - mine
     bf16 = jnp.bfloat16
 
+    other_tokens = lax.ppermute(next_tokens, "c", SWAP)
     local = lax.dot_general(
         tokens_in, cotangent, (((0,), (0,)), ((), ())), preferred_element_type=jnp.float32
     )
@@ -118,6 +111,7 @@
     got = lax.ppermute(give, "c", SWAP)
     pair = rearranged(pair_body, mine, local, got)
     near = summed(exchange(pair.reshape(8, 512, 128), NEAR)).astype(bf16)
+    near, other_tokens = lax.optimization_barrier((near, other_tokens))
     gradient = summed(exchange(near.reshape(64, 8, 128), FAR))
 
     new_first = beta_one * first_moment + (1.0 - beta_one) * gradient
@@ -132,9 +126,9 @@
     far = exchange(jnp.broadcast_to(low_weight, (64, 8, 128)), FAR).reshape(512, 128)
     near = exchange(jnp.broadcast_to(far, (8, 512, 128)), NEAR)
     near = near.reshape(8, 4, 16, 8, 128)
-    other = lax.ppermute(near, "c", SWAP)
-    own_part = half_forward(mine, next_tokens, near, None, jnp.float32)
-    next_out = half_forward(theirs, next_tokens, other, own_part, bf16)
+    for_other = half_forward(mine, other_tokens, near)
+    from_other = lax.ppermute(for_other, "c", SWAP)
+    next_out = (half_forward(mine, next_tokens, near) + from_other).astype(bf16)
     return (new_master, new_first, new_second, next_out)
 
 

time: 117 us -> 121 us (1.034)
  blocking collectives: 83.4 us -> 63.8 us
  waiting for transfers between devices: 4.21 us -> 17 us
  starting transfers between devices: 22.1 us -> 29.4 us
  other arithmetic: 0.84 us -> 2.67 us
  Pallas kernels: 1.62 us -> 3.26 us
    all_to_all x4 -> x3, blocking collectives: 83.4 us -> 63.8 us  [exchange(): return lax.all_to_all(value, axes, 0, 0, tiled=True)]
    all_to_all x0 -> x1, waiting for transfers between devices: none -> 14.2 us  [exchange(): return lax.all_to_all(value, axes, 0, 0, tiled=True)]
    all_to_all x0 -> x1, starting transfers between devices: none -> 4.38 us  [exchange(): return lax.all_to_all(value, axes, 0, 0, tiled=True)]
    ppermute x1 -> x2, starting transfers between devices: 6.12 us -> 9 us  [the longest x1 6.71 us: on_device(): from_other = lax.ppermute(for_other, 'c', SWAP)]
    ppermute x1 -> x2, waiting for transfers between devices: 1.95 us -> 0.53 us  [the longest x1 0.53 us: on_device(): from_other = lax.ppermute(for_other, 'c', SWAP)]
    reduce_sum x2, other arithmetic: 0.22 us -> 1.44 us  [summed(): return jnp.sum(value.astype(jnp.float32), axis=0)]
  transfers between devices with their start and end apart: 2 -> 4, of which waited for: 2 -> 3; matrix products, arithmetic and copies ran while one was open for 0% -> 1% of each run, Pallas kernels for 0% -> 0%
where the time goes in v4:
time: 121 us; the launch traced here: 120 us
  blocking collectives  63.8 us (53%)
  starting transfers between devices  29.4 us (24%)
  waiting for transfers between devices  17 us (14%)
  Pallas kernels  3.26 us (3%)
  other arithmetic  2.67 us (2%)
  local copies, waits for them, and re-layouts  1.75 us (1%)
  matrix products  1.51 us (1%)
    all_to_all x3, blocking collectives, exchange(): return lax.all_to_all(value, axes, 0, 0, tiled=True)  63.8 us
    ppermute x1, starting transfers between devices, on_device(): got = lax.ppermute(give, 'c', SWAP)  16 us
    all_to_all x1, waiting for transfers between devices, exchange(): return lax.all_to_all(value, axes, 0, 0, tiled=True)  14.2 us
    ppermute x1, starting transfers between devices, on_device(): from_other = lax.ppermute(for_other, 'c', SWAP)  6.71 us
    all_to_all x1, starting transfers between devices, exchange(): return lax.all_to_all(value, axes, 0, 0, tiled=True)  4.38 us
  transfers between devices with their start and end apart: 4, of which 3 were waited for; matrix products, arithmetic and copies ran while one was open for 1% of the time, Pallas kernels for 0%

profile of v4, /device:TPU:1, one launch (start us, length us, event | category | flops | bytes accessed | tf_op | source)
XLA Modules:
  0.0 120.1 jit_solution(836643742814992519)
XLA Ops:
  0.6 0.0 copy-start
  0.7 1.6 %copy-done = bf16[128,8192]{1,0:T(8,128)(2,1)S(1)} copy-done((bf16[128,8192]{1,0:T(8,128)(2,1)S(1)}, bf16[128,8192]{1,0:T(8,128)(2,1)}, u32[]{:S(2)}) %copy-start) | copy-done | bytes 2097176
  2.2 1.5 %fusion.3.gradient_ref = f32[8192,128]{1,0:T(8,128)S(1)} fusion(bf16[128,8192]{1,0:T(8,128)(2,1)S(1)} %copy-done, bf16[128,128]{1,0:T(8,128)(2,1)} %param.7), kind=kOutput, calls=%fused_computation.7 | convolution fusion | flops 268435456 | bytes 6324224 | tf_op jit(solution)/shard_map/dot_general | solution.py:107
  3.7 0.1 shard_map.93
  3.9 16.0 %collective-permute-start = (bf16[8,4,16,8,128]{4,3,2,1,0:T(8,128)(2,1)S(1)}, bf16[8,4,16,8,128]{4,3,2,1,0:T(8,128)(2,1)S(1)}, u32[]{:S(2)}, u32[]{:S(2)}) collective-permute-start(bf16[8,4,16,8,128]{4,3,2,1,0:T(8,128)(2,1)S(1)} %shard_map.93), channel_id=1, source_target_pairs={{0,128},{128,0},{1,129},{129,1},{2,130},{130,2},{3,131},{131,3},{4... | collective-permute-start | bytes 3145736 | tf_op jit(solution)/shard_map/ppermute | solution.py:111
  19.9 2.3 %collective-permute-done.got_ref = bf16[8,4,16,8,128]{4,3,2,1,0:T(8,128)(2,1)S(1)} collective-permute-done((bf16[8,4,16,8,128]{4,3,2,1,0:T(8,128)(2,1)S(1)}, bf16[8,4,16,8,128]{4,3,2,1,0:T(8,128)(2,1)S(1)}, u32[]{:S(2)}, u32[]{:S(2)}) %collective-permute-start) | collective-permute-done | bytes 1048608 | tf_op jit(solution)/shard_map/ppermute | solution.py:111
  22.2 1.3 %shard_map.94 = bf16[8,4,16,8,128]{4,3,2,1,0:T(8,128)(2,1)} custom-call(s32[1]{0:T(128)} %bitcast.half_ref, f32[8192,128]{1,0:T(8,128)S(1)} %fusion.3.gradient_ref, bf16[8,4,16,8,128]{4,3,2,1,0:T(8,128)(2,1)S(1)} %collective-permute-done.got_ref), custom_call_target="tpu_custom_call" | custom-call | tf_op jit(solution)/shard_map/pallas_call | solution.py:54
  23.5 0.0 copy-start.1
  23.5 0.0 copy-start.2
  23.5 0.0 copy-start.3
  23.5 0.0 copy-start.4
  23.5 4.4 %all-to-all-start = ((bf16[8,512,128]{2,1,0:T(8,128)(2,1)}), bf16[8,512,128]{2,1,0:T(8,128)(2,1)}, u32[]{:S(2)}, u32[]{:S(2)}) async-start(bf16[8,512,128]{2,1,0:T(8,128)(2,1)} %bitcast.1), calls=%async_computation | async-start | bytes 2097152 | tf_op jit(solution)/shard_map/all_to_all | solution.py:93
  27.9 0.0 copy-done.1
  27.9 2.3 %collective-permute-start.1 = (bf16[64,8192]{1,0:T(8,128)(2,1)S(1)}, bf16[64,8192]{1,0:T(8,128)(2,1)}, u32[]{:S(2)}, u32[]{:S(2)}) collective-permute-start(bf16[64,8192]{1,0:T(8,128)(2,1)S(1)} %copy-done.1), channel_id=1, source_target_pairs={{0,128},{128,0},{1,129},{129,1},{2,130},{130,2},{3,131},{131,3},{4... | collective-permute-start | bytes 3145736 | tf_op jit(solution)/shard_map/ppermute | solution.py:106
  30.2 14.2 %all-to-all-done = bf16[8,512,128]{2,1,0:T(8,128)(2,1)} async-done(((bf16[8,512,128]{2,1,0:T(8,128)(2,1)}), bf16[8,512,128]{2,1,0:T(8,128)(2,1)}, u32[]{:S(2)}, u32[]{:S(2)}) %all-to-all-start) | async-done | bytes 1048608 | tf_op jit(solution)/shard_map/all_to_all | solution.py:93
  44.4 1.4 %reduce_sum.21 = bf16[512,128]{1,0:T(8,128)(2,1)S(1)} reduce(bf16[8,512,128]{2,1,0:T(8,128)(2,1)} %all-to-all-done, bf16[]{:T(256)} %constant.9.clone.1), dimensions={0}, to_apply=%region_0.0 | reduce | flops 458752 | bytes 1179650 | tf_op jit(solution)/shard_map/reduce_sum | solution.py:97
  45.8 0.0 collective-permute-done.1.tokens_ref
  45.8 30.0 %all_to_all.20 = bf16[64,8,128]{2,1,0:T(8,128)(2,1)S(1)} all-to-all(bf16[64,8,128]{2,1,0:T(8,128)(2,1)S(1)} %bitcast.9), channel_id=1, replica_groups=mesh['yh'=4,'c'=2,'zh'=4,'zl'=2,'xh'=4,'xl'=2,'yl'=2] {'yh','zh','xh'}, dimensions={0} | all-to-all | bytes 262144 | tf_op jit(solution)/shard_map/all_to_all | solution.py:93
  75.8 0.1 convert_reduce_fusion
  75.9 0.0 copy-done.2
  75.9 0.0 copy-done.3
  75.9 0.0 copy-done.4
  75.9 0.6 fusion.1
  76.5 19.7 %all_to_all.21 = bf16[64,8,128]{2,1,0:T(8,128)(2,1)S(1)} all-to-all(bf16[64,8,128]{2,1,0:T(8,128)(2,1)S(1)} %broadcast_in_dim.6), channel_id=1, replica_groups=mesh['yh'=4,'c'=2,'zh'=4,'zl'=2,'xh'=4,'xl'=2,'yl'=2] {'yh','zh','xh'}, dimensions={0} | all-to-all | bytes 262144 | tf_op jit(solution)/shard_map/all_to_all | solution.py:93
  96.3 0.1 broadcast_in_dim.7
  96.4 14.0 %all_to_all.22 = bf16[8,512,128]{2,1,0:T(8,128)(2,1)S(1)} all-to-all(bf16[8,512,128]{2,1,0:T(8,128)(2,1)S(1)} %broadcast_in_dim.7), channel_id=1, replica_groups=mesh['yh'=4,'c'=2,'zh'=4,'zl'=2,'xh'=4,'xl'=2,'yl'=2] {'zl','xl','yl'}, dimensions={0} | all-to-all | bytes 2097152 | tf_op jit(solution)/shard_map/all_to_all | solution.py:93
  110.4 1.5 %shard_map.96 = f32[64,128]{1,0:T(8,128)S(1)} custom-call(s32[1]{0:T(128)} %bitcast.half_ref, bf16[64,8192]{1,0:T(8,128)(2,1)} %collective-permute-done.1.tokens_ref, bf16[8,4,16,8,128]{4,3,2,1,0:T(8,128)(2,1)S(1)} %bitcast.7), custom_call_target="tpu_custom_call" | custom-call | tf_op jit(solution)/shard_map/pallas_call | solution.py:82
  112.0 6.7 %collective-permute-start.2 = (f32[64,128]{1,0:T(8,128)S(1)}, f32[64,128]{1,0:T(8,128)S(1)}, u32[]{:S(2)}, u32[]{:S(2)}) collective-permute-start(f32[64,128]{1,0:T(8,128)S(1)} %shard_map.96), channel_id=1, source_target_pairs={{0,128},{128,0},{1,129},{129,1},{2,130},{130,2},{3,131},{131,3},{4... | collective-permute-start | bytes 98312 | tf_op jit(solution)/shard_map/ppermute | solution.py:130
  118.7 0.3 shard_map.95
  119.0 0.5 collective-permute-done.2
  119.5 0.6 add_convert_fusion
  (1 shorter events, 0.0 us)
Async XLA Ops:
  0.6 1.6 %copy-start = (bf16[128,8192]{1,0:T(8,128)(2,1)S(1)}, bf16[128,8192]{1,0:T(8,128)(2,1)}, u32[]{:S(2)}) copy-start(bf16[128,8192]{1,0:T(8,128)(2,1)} %param.6) | copy-start | bytes 6291460
  3.9 18.3 %collective-permute-start = (bf16[8,4,16,8,128]{4,3,2,1,0:T(8,128)(2,1)S(1)}, bf16[8,4,16,8,128]{4,3,2,1,0:T(8,128)(2,1)S(1)}, u32[]{:S(2)}, u32[]{:S(2)}) collective-permute-start(bf16[8,4,16,8,128]{4,3,2,1,0:T(8,128)(2,1)S(1)} %shard_map.93), channel_id=1, source_target_pairs={{0,128},{128,0},{1,129},{129,1},{2,130},{130,2},{3,131},{131,3},{4... | collective-permute-start | bytes 3145736 | tf_op jit(solution)/shard_map/ppermute | solution.py:111
  23.5 4.4 %copy-start.1 = (bf16[64,8192]{1,0:T(8,128)(2,1)S(1)}, bf16[64,8192]{1,0:T(8,128)(2,1)}, u32[]{:S(2)}) copy-start(bf16[64,8192]{1,0:T(8,128)(2,1)} %tokens_ref.1) | copy-start | bytes 3145732
  23.5 52.4 %copy-start.2 = (f32[8,128]{1,0:T(8,128)S(1)}, f32[8,128]{1,0:T(8,128)}, u32[]{:S(2)}) copy-start(f32[8,128]{1,0:T(8,128)} %param.9) | copy-start | bytes 12292
  23.5 52.4 %copy-start.3 = (f32[8,128]{1,0:T(8,128)S(1)}, f32[8,128]{1,0:T(8,128)}, u32[]{:S(2)}) copy-start(f32[8,128]{1,0:T(8,128)} %param.10) | copy-start | bytes 12292
  23.5 52.4 %copy-start.4 = (f32[8,128]{1,0:T(8,128)S(1)}, f32[8,128]{1,0:T(8,128)}, u32[]{:S(2)}) copy-start(f32[8,128]{1,0:T(8,128)} %param.11) | copy-start | bytes 12292
  23.5 20.9 %all-to-all-start = ((bf16[8,512,128]{2,1,0:T(8,128)(2,1)}), bf16[8,512,128]{2,1,0:T(8,128)(2,1)}, u32[]{:S(2)}, u32[]{:S(2)}) async-start(bf16[8,512,128]{2,1,0:T(8,128)(2,1)} %bitcast.1), calls=%async_computation | async-start | bytes 2097152 | tf_op jit(solution)/shard_map/all_to_all | solution.py:93
  27.9 17.9 %collective-permute-start.1 = (bf16[64,8192]{1,0:T(8,128)(2,1)S(1)}, bf16[64,8192]{1,0:T(8,128)(2,1)}, u32[]{:S(2)}, u32[]{:S(2)}) collective-permute-start(bf16[64,8192]{1,0:T(8,128)(2,1)S(1)} %copy-done.1), channel_id=1, source_target_pairs={{0,128},{128,0},{1,129},{129,1},{2,130},{130,2},{3,131},{131,3},{4... | collective-permute-start | bytes 3145736 | tf_op jit(solution)/shard_map/ppermute | solution.py:106
  112.0 7.6 %collective-permute-start.2 = (f32[64,128]{1,0:T(8,128)S(1)}, f32[64,128]{1,0:T(8,128)S(1)}, u32[]{:S(2)}, u32[]{:S(2)}) collective-permute-start(f32[64,128]{1,0:T(8,128)S(1)} %shard_map.96), channel_id=1, source_target_pairs={{0,128},{128,0},{1,129},{129,1},{2,130},{130,2},{3,131},{131,3},{4... | collective-permute-start | bytes 98312 | tf_op jit(solution)/shard_map/ppermute | solution.py:130

commit v5 on v4

--- a/solution.py
+++ b/solution.py
@@ -86,7 +86,7 @@
         out_specs=VMEM,
         compiler_params=pltpu.CompilerParams(vmem_limit_bytes=16 << 20),
         interpret=INTERPRET,
-    )(half, held(next_tokens), held(weight))
+    )(half, next_tokens, held(weight))
 
 
 def exchange(value, axes):
@@ -109,9 +109,9 @@
     )
     give = rearranged(give_body, theirs, local)
     got = lax.ppermute(give, "c", SWAP)
+    got, other_tokens = lax.optimization_barrier((got, other_tokens))
     pair = rearranged(pair_body, mine, local, got)
     near = summed(exchange(pair.reshape(8, 512, 128), NEAR)).astype(bf16)
-    near, other_tokens = lax.optimization_barrier((near, other_tokens))
     gradient = summed(exchange(near.reshape(64, 8, 128), FAR))
 
     new_first = beta_one * first_moment + (1.0 - beta_one) * gradient

time: 121 us -> 120 us (level)
  blocking collectives: 63.8 us -> 83.5 us
  waiting for transfers between devices: 17 us -> 3.15 us
  starting transfers between devices: 29.4 us -> 24.2 us
  Pallas kernels: 3.26 us -> 0.95 us
    all_to_all x3 -> x4, blocking collectives: 63.8 us -> 83.5 us  [exchange(): return lax.all_to_all(value, axes, 0, 0, tiled=True)]
    all_to_all x1 -> x0, waiting for transfers between devices: 14.2 us -> none  [exchange(): return lax.all_to_all(value, axes, 0, 0, tiled=True)]
    all_to_all x1 -> x0, starting transfers between devices: 4.38 us -> none  [exchange(): return lax.all_to_all(value, axes, 0, 0, tiled=True)]
    ppermute x1, waiting for transfers between devices: 0.01 us -> 2.3 us  [on_device(): other_tokens = lax.ppermute(next_tokens, 'c', SWAP)]
    ppermute x1, waiting for transfers between devices: 2.26 us -> 0.33 us  [on_device(): got = lax.ppermute(give, 'c', SWAP)]
    pallas_call x2, Pallas kernels: 1.84 us -> 0.6 us  [half_forward(): pl.pallas_call(forward_body, out_shape=in_vmem((next_tokens.shape[0], 128...]
  transfers between devices with their start and end apart: 4 -> 3, of which waited for: 3 -> 3; matrix products, arithmetic and copies ran while one was open for 1% -> 0% of each run, Pallas kernels for 0% -> 0%
where the time goes in v5:
time: 120 us; the launch traced here: 119 us
  blocking collectives  83.5 us (70%)
  starting transfers between devices  24.2 us (20%)
  waiting for transfers between devices  3.15 us (3%)
  other arithmetic  2.67 us (2%)
  local copies, waits for them, and re-layouts  2.52 us (2%)
  matrix products  1.5 us (1%)
    all_to_all x4, blocking collectives, exchange(): return lax.all_to_all(value, axes, 0, 0, tiled=True)  83.5 us
    ppermute x1, starting transfers between devices, on_device(): got = lax.ppermute(give, 'c', SWAP)  16.2 us
    ppermute x1, starting transfers between devices, on_device(): from_other = lax.ppermute(for_other, 'c', SWAP)  6.09 us
  transfers between devices with their start and end apart: 3, of which 3 were waited for; matrix products, arithmetic and copies ran while one was open for 0% of the time, Pallas kernels for 0%

profile of v5, /device:TPU:1, one launch (start us, length us, event | category | flops | bytes accessed | tf_op | source)
XLA Modules:
  0.0 119.3 jit_solution(1769954584465616239)
XLA Ops:
  0.6 0.0 copy-start
  0.7 1.6 %copy-done = bf16[128,8192]{1,0:T(8,128)(2,1)S(1)} copy-done((bf16[128,8192]{1,0:T(8,128)(2,1)S(1)}, bf16[128,8192]{1,0:T(8,128)(2,1)}, u32[]{:S(2)}) %copy-start) | copy-done | bytes 2097176
  2.2 1.5 %fusion.3.gradient_ref = f32[8192,128]{1,0:T(8,128)S(1)} fusion(bf16[128,8192]{1,0:T(8,128)(2,1)S(1)} %copy-done, bf16[128,128]{1,0:T(8,128)(2,1)} %param.7), kind=kOutput, calls=%fused_computation.7 | convolution fusion | flops 268435456 | bytes 6324224 | tf_op jit(solution)/shard_map/dot_general | solution.py:107
  3.7 0.0 copy-start.1
  3.7 0.1 shard_map.93
  3.9 16.2 %collective-permute-start = (bf16[8,4,16,8,128]{4,3,2,1,0:T(8,128)(2,1)S(1)}, bf16[8,4,16,8,128]{4,3,2,1,0:T(8,128)(2,1)S(1)}, u32[]{:S(2)}, u32[]{:S(2)}) collective-permute-start(bf16[8,4,16,8,128]{4,3,2,1,0:T(8,128)(2,1)S(1)} %shard_map.93), channel_id=1, source_target_pairs={{0,128},{128,0},{1,129},{129,1},{2,130},{130,2},{3,131},{131,3},{4... | collective-permute-start | bytes 3145736 | tf_op jit(solution)/shard_map/ppermute | solution.py:111
  20.1 0.0 copy-done.1
  20.1 1.9 %collective-permute-start.1 = (bf16[64,8192]{1,0:T(8,128)(2,1)S(1)}, bf16[64,8192]{1,0:T(8,128)(2,1)S(1)}, u32[]{:S(2)}, u32[]{:S(2)}) collective-permute-start(bf16[64,8192]{1,0:T(8,128)(2,1)S(1)} %copy-done.1), channel_id=1, source_target_pairs={{0,128},{128,0},{1,129},{129,1},{2,130},{130,2},{3,131},{131,3},{4... | collective-permute-start | bytes 3145736 | tf_op jit(solution)/shard_map/ppermute | solution.py:106
  22.0 0.3 collective-permute-done.got_ref
  22.3 2.3 %collective-permute-done.1.tokens_ref = bf16[64,8192]{1,0:T(8,128)(2,1)S(1)} collective-permute-done((bf16[64,8192]{1,0:T(8,128)(2,1)S(1)}, bf16[64,8192]{1,0:T(8,128)(2,1)S(1)}, u32[]{:S(2)}, u32[]{:S(2)}) %collective-permute-start.1) | collective-permute-done | bytes 1048608 | tf_op jit(solution)/shard_map/ppermute | solution.py:106
  24.6 0.0 copy-start.2
  24.6 0.2 shard_map.94
  24.8 0.8 copy-done.2
  25.6 0.0 copy-start.4
  25.6 18.3 %all_to_all.20 = bf16[8,512,128]{2,1,0:T(8,128)(2,1)} all-to-all(bf16[8,512,128]{2,1,0:T(8,128)(2,1)S(1)} %bitcast.9), channel_id=1, replica_groups=mesh['yh'=4,'c'=2,'zh'=4,'zl'=2,'xh'=4,'xl'=2,'yl'=2] {'zl','xl','yl'}, dimensions={0} | all-to-all | bytes 2097152 | tf_op jit(solution)/shard_map/all_to_all | solution.py:93
  43.9 1.4 %reduce_sum.21 = bf16[512,128]{1,0:T(8,128)(2,1)S(1)} reduce(bf16[8,512,128]{2,1,0:T(8,128)(2,1)} %all_to_all.20, bf16[]{:T(256)} %constant.9.clone.1), dimensions={0}, to_apply=%region_0.0 | reduce | flops 458752 | bytes 1179650 | tf_op jit(solution)/shard_map/reduce_sum | solution.py:97
  45.3 0.0 copy-start.3
  45.3 30.5 %all_to_all.21 = bf16[64,8,128]{2,1,0:T(8,128)(2,1)S(1)} all-to-all(bf16[64,8,128]{2,1,0:T(8,128)(2,1)S(1)} %bitcast.10), channel_id=1, replica_groups=mesh['yh'=4,'c'=2,'zh'=4,'zl'=2,'xh'=4,'xl'=2,'yl'=2] {'yh','zh','xh'}, dimensions={0} | all-to-all | bytes 262144 | tf_op jit(solution)/shard_map/all_to_all | solution.py:93
  75.8 0.1 convert_reduce_fusion
  75.8 0.0 copy-done.4
  75.8 0.0 copy-done.5
  75.8 0.0 copy-done.6
  75.8 0.6 fusion.1
  76.5 19.7 %all_to_all.22 = bf16[64,8,128]{2,1,0:T(8,128)(2,1)S(1)} all-to-all(bf16[64,8,128]{2,1,0:T(8,128)(2,1)S(1)} %broadcast_in_dim.6), channel_id=1, replica_groups=mesh['yh'=4,'c'=2,'zh'=4,'zl'=2,'xh'=4,'xl'=2,'yl'=2] {'yh','zh','xh'}, dimensions={0} | all-to-all | bytes 262144 | tf_op jit(solution)/shard_map/all_to_all | solution.py:93
  96.2 0.1 broadcast_in_dim.7
  96.3 15.1 %all_to_all.23 = bf16[8,512,128]{2,1,0:T(8,128)(2,1)S(1)} all-to-all(bf16[8,512,128]{2,1,0:T(8,128)(2,1)S(1)} %broadcast_in_dim.7), channel_id=1, replica_groups=mesh['yh'=4,'c'=2,'zh'=4,'zl'=2,'xh'=4,'xl'=2,'yl'=2] {'zl','xl','yl'}, dimensions={0} | all-to-all | bytes 2097152 | tf_op jit(solution)/shard_map/all_to_all | solution.py:93
  111.4 0.0 copy-done.3
  111.4 0.3 shard_map.96
  111.7 6.1 %collective-permute-start.2 = (f32[64,128]{1,0:T(8,128)S(1)}, f32[64,128]{1,0:T(8,128)S(1)}, u32[]{:S(2)}, u32[]{:S(2)}) collective-permute-start(f32[64,128]{1,0:T(8,128)S(1)} %shard_map.96), channel_id=1, source_target_pairs={{0,128},{128,0},{1,129},{129,1},{2,130},{130,2},{3,131},{131,3},{4... | collective-permute-start | bytes 98312 | tf_op jit(solution)/shard_map/ppermute | solution.py:130
  117.8 0.3 shard_map.95
  118.1 0.5 collective-permute-done.2
  118.6 0.6 add_convert_fusion
  (3 shorter events, 0.0 us)
Async XLA Ops:
  0.6 1.6 %copy-start = (bf16[128,8192]{1,0:T(8,128)(2,1)S(1)}, bf16[128,8192]{1,0:T(8,128)(2,1)}, u32[]{:S(2)}) copy-start(bf16[128,8192]{1,0:T(8,128)(2,1)} %param.6) | copy-start | bytes 6291460
  3.7 16.3 %copy-start.1 = (bf16[64,8192]{1,0:T(8,128)(2,1)S(1)}, bf16[64,8192]{1,0:T(8,128)(2,1)}, u32[]{:S(2)}) copy-start(bf16[64,8192]{1,0:T(8,128)(2,1)} %tokens_ref.1) | copy-start | bytes 3145732
  3.9 18.4 %collective-permute-start = (bf16[8,4,16,8,128]{4,3,2,1,0:T(8,128)(2,1)S(1)}, bf16[8,4,16,8,128]{4,3,2,1,0:T(8,128)(2,1)S(1)}, u32[]{:S(2)}, u32[]{:S(2)}) collective-permute-start(bf16[8,4,16,8,128]{4,3,2,1,0:T(8,128)(2,1)S(1)} %shard_map.93), channel_id=1, source_target_pairs={{0,128},{128,0},{1,129},{129,1},{2,130},{130,2},{3,131},{131,3},{4... | collective-permute-start | bytes 3145736 | tf_op jit(solution)/shard_map/ppermute | solution.py:111
  20.1 4.6 %collective-permute-start.1 = (bf16[64,8192]{1,0:T(8,128)(2,1)S(1)}, bf16[64,8192]{1,0:T(8,128)(2,1)S(1)}, u32[]{:S(2)}, u32[]{:S(2)}) collective-permute-start(bf16[64,8192]{1,0:T(8,128)(2,1)S(1)} %copy-done.1), channel_id=1, source_target_pairs={{0,128},{128,0},{1,129},{129,1},{2,130},{130,2},{3,131},{131,3},{4... | collective-permute-start | bytes 3145736 | tf_op jit(solution)/shard_map/ppermute | solution.py:106
  24.6 1.0 copy-start.2
  25.6 50.2 %copy-start.4 = (f32[8,128]{1,0:T(8,128)S(1)}, f32[8,128]{1,0:T(8,128)}, u32[]{:S(2)}) copy-start(f32[8,128]{1,0:T(8,128)} %param.9) | copy-start | bytes 12292
  25.6 50.2 %copy-start.5 = (f32[8,128]{1,0:T(8,128)S(1)}, f32[8,128]{1,0:T(8,128)}, u32[]{:S(2)}) copy-start(f32[8,128]{1,0:T(8,128)} %param.10) | copy-start | bytes 12292
  25.6 50.2 %copy-start.6 = (f32[8,128]{1,0:T(8,128)S(1)}, f32[8,128]{1,0:T(8,128)}, u32[]{:S(2)}) copy-start(f32[8,128]{1,0:T(8,128)} %param.11) | copy-start | bytes 12292
  45.3 66.1 %copy-start.3 = (bf16[64,8192]{1,0:T(8,128)(2,1)S(1)}, bf16[64,8192]{1,0:T(8,128)(2,1)}, u32[]{:S(2)}) copy-start(bf16[64,8192]{1,0:T(8,128)(2,1)} %copy-done.2) | copy-start | bytes 3145732
  111.7 6.9 %collective-permute-start.2 = (f32[64,128]{1,0:T(8,128)S(1)}, f32[64,128]{1,0:T(8,128)S(1)}, u32[]{:S(2)}, u32[]{:S(2)}) collective-permute-start(f32[64,128]{1,0:T(8,128)S(1)} %shard_map.96), channel_id=1, source_target_pairs={{0,128},{128,0},{1,129},{129,1},{2,130},{130,2},{3,131},{131,3},{4... | collective-permute-start | bytes 98312 | tf_op jit(solution)/shard_map/ppermute | solution.py:130
